TPU v7x, 32 devices: a whole 2x2x4 slice. The times are simulated.
32 devices in a mesh: comp: 4 (over y, core), tile: 8 (over z, x).
Axes of the slice: x: 2, y: 2, z: 4, core: 2. Of those that a mesh axis runs over, the one named last changes fastest.
Arguments:
- state: float32 [2, 8, 256, 4096], P(None, None, 'comp', 'tile'), may hold values from -6 to 6
- courant: float32 [8, 256], P(None, 'comp'), may hold values from -0.9 to 0.9
- mixing: float32 [7, 256], P(None, 'comp'), may hold values from 0.05 to 0.24
- exchange_coef: float32 [256, 4096], P('comp', 'tile'), may hold values from 0.2 to 0.8
- sea_mask: int32 [256, 4096], P('comp', 'tile'), may hold values 0 or 1
- margin_count: int32 [4, 8, 3, 4], P('comp', 'tile'), may hold values from 0 to 4096, as said below
- margin_row: int32 [4, 8, 3, 4, 4096], P('comp', 'tile'), may hold values from 0 to 63
- margin_col: int32 [4, 8, 3, 4, 4096], P('comp', 'tile'), may hold values from 0 to 511, as said below
- margin_weight: float32 [4, 8, 3, 4, 4096], P('comp', 'tile'), may hold values from 0.05 to 0.6
Outputs:
- new_state: float32 [2, 8, 256, 4096], P(None, None, 'comp', 'tile')
- partner_surface: float32 [2, 256, 4096], P(None, 'comp', 'tile')
Inputs may be any that keep to these rules, and one draw needn't show every extreme that they name: margin_count[g, t, o, h] equals margin_count[h, (t + o - 1) mod 8, 2 - o, g], and row r of the one list is the same margin as row r of the other. Only pairs of one atmosphere device (comp index below 3) and one ocean device have rows: an atmosphere device couples with the three ocean devices at tile offsets -1, 0 and 1, an ocean device with the atmosphere devices at those offsets; every such pair has at least 3584 rows. `margin_col`: for list index o = 0 (partner to the west) the columns lie below 128, for o = 2 (partner to the east) at 384 or above.
All inputs are finite; a program needn't handle non-finite values. No bound on the sum of `sea_mask` on one device may be relied on, other than what follows from the above.
Results may differ from a plain program's by a relative error of at most 0.0003.
Values sent between devices are 32-bit elements; how exact they have to be, the bound alone decides.
A program may use at most 64 MiB of HBM per device.

v0:
```python
import jax
import jax.numpy as jnp
from jax import lax
from jax.sharding import PartitionSpec as P

SUBSTEPS = 2


def with_halo(block, sides, width):
    for axis, dim in sides:
        count = lax.axis_size(axis)
        forward = [(i, i + 1) for i in range(count - 1)]
        forward.append((count - 1, 0))
        backward = [(target, source) for source, target in forward]
        low = lax.ppermute(
            lax.slice_in_dim(block, block.shape[dim] - width, None, axis=dim), axis, forward
        )
        high = lax.ppermute(lax.slice_in_dim(block, 0, width, axis=dim), axis, backward)
        block = jnp.concatenate([low, block, high], axis=dim)
    return block


def transport(padded, speed):
    left = padded[..., :-2]
    middle = padded[..., 1:-1]
    right = padded[..., 2:]
    return (
        middle - 0.5 * speed * (right - left) + 0.5 * speed * speed * (right - 2.0 * middle + left)
    )


def vertical_mix(field, coeff):
    jump_up = field[:, 1:] - field[:, :-1]
    flux = coeff[None, :, :, None] * jump_up
    empty = jnp.zeros_like(flux[:, :1])
    upper = jnp.concatenate([flux, empty], axis=1)
    lower = jnp.concatenate([empty, flux], axis=1)
    return field + upper - lower


def shards(
    state,
    courant,
    mixing,
    exchange_coef,
    sea_mask,
    margin_count,
    margin_row,
    margin_col,
    margin_weight,
):
    field_count, level_count, row_count, col_count = state.shape
    slot_count = margin_row.shape[-1]
    comp_peers = margin_row.shape[3]
    list_count = 3 * comp_peers
    tile_total = lax.axis_size("tile")
    tile_here = lax.axis_index("tile")
    surface_rows = state[:, 0].reshape(field_count * row_count, col_count)
    row_lists = margin_row.reshape(list_count, slot_count)
    col_lists = margin_col.reshape(list_count, slot_count)
    counts = margin_count.reshape(list_count)
    row_iota = jnp.arange(row_count, dtype=jnp.int32)[:, None]
    col_iota = jnp.arange(col_count, dtype=jnp.int32)[:, None]
    slot_iota = jnp.arange(slot_count, dtype=jnp.int32)

    def pick_list(carry, parts):
        row_list, col_list, count_one = parts
        col_table = (col_iota == col_list[None, :]).astype(jnp.float32)
        picked = jnp.dot(
            surface_rows,
            col_table,
            precision=lax.Precision.HIGHEST,
            preferred_element_type=jnp.float32,
        )
        picked = picked.reshape(field_count, row_count, slot_count)
        row_match = row_iota == row_list[None, :]
        values = jnp.sum(jnp.where(row_match[None], picked, 0.0), axis=1)
        values = jnp.where((slot_iota < count_one)[None, :], values, 0.0)
        return (carry, values)

    unused, picked_all = lax.scan(pick_list, 0, (row_lists, col_lists, counts))
    outgoing = jnp.transpose(
        picked_all.reshape(3, comp_peers, field_count, slot_count), (2, 0, 1, 3)
    )
    partner_tiles = (tile_here + jnp.arange(3, dtype=jnp.int32) - 1) % tile_total
    tile_table = partner_tiles[:, None] == jnp.arange(tile_total, dtype=jnp.int32)[None, :]
    spread = jnp.where(tile_table[None, :, None, :, None], outgoing[:, :, :, None, :], 0.0)
    blocks = jnp.sum(spread, axis=1).reshape(field_count, comp_peers * tile_total, slot_count)
    arrived = lax.all_to_all(blocks, ("comp", "tile"), split_axis=1, concat_axis=1, tiled=True)
    arrived = arrived.reshape(field_count, comp_peers, tile_total, slot_count)
    chosen = jnp.where(tile_table[None, :, None, :, None], arrived[:, None], 0.0)
    incoming = jnp.sum(chosen, axis=3)
    speed = courant[:, :, None]
    field = state
    padded = with_halo(field, (("tile", 3),), SUBSTEPS)
    for step in range(SUBSTEPS):
        padded = vertical_mix(transport(padded, speed), mixing)
    field = padded
    weights = margin_weight.reshape(3, comp_peers, slot_count)
    terms = jnp.transpose(
        (incoming * weights[None]).reshape(field_count, list_count, slot_count), (1, 0, 2)
    )

    def land_list(total, parts):
        row_list, col_list, term_one = parts
        col_table = (col_iota == col_list[None, :]).astype(jnp.float32)
        row_match = row_iota == row_list[None, :]
        spread = jnp.where(row_match[None], term_one[:, None, :], 0.0).reshape(
            field_count * row_count, slot_count
        )
        landed = lax.dot_general(
            spread,
            col_table,
            (((1,), (1,)), ((), ())),
            precision=lax.Precision.HIGHEST,
            preferred_element_type=jnp.float32,
        )
        return (total + landed, 0)

    start_total = jnp.zeros((field_count * row_count, col_count), jnp.float32)
    partner, unused_two = lax.scan(land_list, start_total, (row_lists, col_lists, terms))
    partner = partner.reshape(field_count, row_count, col_count)
    ocean = lax.axis_index("comp") == lax.axis_size("comp") - 1
    rate = exchange_coef * sea_mask.astype(jnp.float32)
    first_own = field[0, 0]
    second_own = field[1, 0]
    first_far = partner[0]
    second_far = partner[1]
    new_first = first_own + rate * (first_far - first_own)
    air_second = second_own + rate * (1.2 * first_far - 0.3 * second_far - second_own)
    sea_second = second_own + rate * (1.2 * first_own - second_far)
    new_second = jnp.where(ocean, sea_second, air_second)
    field = field.at[:, 0].set(jnp.stack([new_first, new_second]))
    return (field, partner)


def solution(mesh):
    in_specs = (
        P(None, None, "comp", "tile"),
        P(None, "comp"),
        P(None, "comp"),
        P("comp", "tile"),
        P("comp", "tile"),
        P("comp", "tile", None, None),
        P("comp", "tile", None, None, None),
        P("comp", "tile", None, None, None),
        P("comp", "tile", None, None, None),
    )
    out_specs = (P(None, None, "comp", "tile"), P(None, "comp", "tile"))
    return jax.shard_map(shards, mesh=mesh, in_specs=in_specs, out_specs=out_specs, check_vma=False)
```

profile of v0, /device:TPU:5, one launch (start us, length us, event | category | flops | bytes accessed | tf_op | source)
XLA Modules:
  0.0 176.7 jit_solution(16265510379821095748)
XLA Ops:
  0.7 2.4 %fusion.21 = (f32[2,8,64,2]{3,2,1,0:T(8,128)}, f32[2,8,64,2]{3,2,1,0:T(8,128)}) fusion(f32[2,8,64,512]{3,2,1,0:T(8,128)} %param.15), kind=kLoop, calls=%fused_computation.54 | loop fusion | bytes 32768 | tf_op jit(solution)/shard_map/slice | solution.py:16
  3.1 4.2 %collective-permute-start.1 = (f32[2,8,64,2]{3,2,1,0:T(8,128)}, f32[2,8,64,2]{3,2,1,0:T(8,128)}, u32[]{:S(2)}, u32[]{:S(2)}) collective-permute-start(f32[2,8,64,2]{3,2,1,0:T(8,128)} %get-tuple-element.167), channel_id=1, source_target_pairs={{1,0},{2,1},{3,2},{4,3},{5,4},{6,5},{7,6},{0,7},{9,8},{10,9},{11,1... | collective-permute-start | bytes 24584 | tf_op jit(solution)/shard_map/ppermute | solution.py:18
  7.6 54.5 %while.23 = (s32[]{:T(128)}, f32[12,2,4096]{2,1,0:T(2,128)S(1)}, s32[12]{0:T(128)S(1)}, s32[12,4096]{1,0:T(8,128)S(1)}, s32[12,4096]{1,0:T(8,128)S(1)}, /*index=5*/f32[128,512]{1,0:T(8,128)S(1)}, s32[]{:T(128)}) while((s32[]{:T(128)}, f32[12,2,4096]{2,1,0:T(2,128)S(1)}, s32[12]{0:T(128)S(1)}, s32[12,4096]{1,0:T(8,128)S(1)}, ...), condition=%wide.region_2.3_spmd.clone, body=%wide.region_0.2_spmd.clone.sunk | while | flops 3224637440 | bytes 991333 | solution.py:81
  7.8 3.1 %select_reduce_fusion.4 = f32[2,4096]{1,0:T(2,128)S(1)} fusion(pred[64,4096]{1,0:T(8,128)(4,1)S(1)} %iota_compare_fusion.14, f32[128,512]{1,0:T(8,128)S(1)} %get-tuple-element.265, s32[4096]{0:T(1024)S(1)} %bitcast.76), kind=kOutput, calls=%fused_computation.8.clone.1 | convolution fusion | flops 3224363008 | bytes 573440 | tf_op jit(solution)/shard_map/while/body/eval_jaxpr/dot_general | solution.py:69
  12.3 3.1 %select_reduce_fusion.4 = f32[2,4096]{1,0:T(2,128)S(1)} fusion(pred[64,4096]{1,0:T(8,128)(4,1)S(1)} %iota_compare_fusion.14, f32[128,512]{1,0:T(8,128)S(1)} %get-tuple-element.265, s32[4096]{0:T(1024)S(1)} %bitcast.76), kind=kOutput, calls=%fused_computation.8.clone.1 | convolution fusion | flops 3224363008 | bytes 573440 | tf_op jit(solution)/shard_map/while/body/eval_jaxpr/dot_general | solution.py:69
  15.5 0.6 dynamic_slice.43
  16.9 3.1 %select_reduce_fusion.4 = f32[2,4096]{1,0:T(2,128)S(1)} fusion(pred[64,4096]{1,0:T(8,128)(4,1)S(1)} %iota_compare_fusion.14, f32[128,512]{1,0:T(8,128)S(1)} %get-tuple-element.265, s32[4096]{0:T(1024)S(1)} %bitcast.76), kind=kOutput, calls=%fused_computation.8.clone.1 | convolution fusion | flops 3224363008 | bytes 573440 | tf_op jit(solution)/shard_map/while/body/eval_jaxpr/dot_general | solution.py:69
  20.0 0.6 dynamic_slice.43
  21.4 3.1 %select_reduce_fusion.4 = f32[2,4096]{1,0:T(2,128)S(1)} fusion(pred[64,4096]{1,0:T(8,128)(4,1)S(1)} %iota_compare_fusion.14, f32[128,512]{1,0:T(8,128)S(1)} %get-tuple-element.265, s32[4096]{0:T(1024)S(1)} %bitcast.76), kind=kOutput, calls=%fused_computation.8.clone.1 | convolution fusion | flops 3224363008 | bytes 573440 | tf_op jit(solution)/shard_map/while/body/eval_jaxpr/dot_general | solution.py:69
  24.5 0.6 dynamic_slice.43
  26.0 3.1 %select_reduce_fusion.4 = f32[2,4096]{1,0:T(2,128)S(1)} fusion(pred[64,4096]{1,0:T(8,128)(4,1)S(1)} %iota_compare_fusion.14, f32[128,512]{1,0:T(8,128)S(1)} %get-tuple-element.265, s32[4096]{0:T(1024)S(1)} %bitcast.76), kind=kOutput, calls=%fused_computation.8.clone.1 | convolution fusion | flops 3224363008 | bytes 573440 | tf_op jit(solution)/shard_map/while/body/eval_jaxpr/dot_general | solution.py:69
  29.1 0.6 dynamic_slice.43
  30.5 3.1 %select_reduce_fusion.4 = f32[2,4096]{1,0:T(2,128)S(1)} fusion(pred[64,4096]{1,0:T(8,128)(4,1)S(1)} %iota_compare_fusion.14, f32[128,512]{1,0:T(8,128)S(1)} %get-tuple-element.265, s32[4096]{0:T(1024)S(1)} %bitcast.76), kind=kOutput, calls=%fused_computation.8.clone.1 | convolution fusion | flops 3224363008 | bytes 573440 | tf_op jit(solution)/shard_map/while/body/eval_jaxpr/dot_general | solution.py:69
  33.6 0.6 dynamic_slice.43
  35.0 3.1 %select_reduce_fusion.4 = f32[2,4096]{1,0:T(2,128)S(1)} fusion(pred[64,4096]{1,0:T(8,128)(4,1)S(1)} %iota_compare_fusion.14, f32[128,512]{1,0:T(8,128)S(1)} %get-tuple-element.265, s32[4096]{0:T(1024)S(1)} %bitcast.76), kind=kOutput, calls=%fused_computation.8.clone.1 | convolution fusion | flops 3224363008 | bytes 573440 | tf_op jit(solution)/shard_map/while/body/eval_jaxpr/dot_general | solution.py:69
  38.2 0.6 dynamic_slice.43
  39.6 3.1 %select_reduce_fusion.4 = f32[2,4096]{1,0:T(2,128)S(1)} fusion(pred[64,4096]{1,0:T(8,128)(4,1)S(1)} %iota_compare_fusion.14, f32[128,512]{1,0:T(8,128)S(1)} %get-tuple-element.265, s32[4096]{0:T(1024)S(1)} %bitcast.76), kind=kOutput, calls=%fused_computation.8.clone.1 | convolution fusion | flops 3224363008 | bytes 573440 | tf_op jit(solution)/shard_map/while/body/eval_jaxpr/dot_general | solution.py:69
  42.7 0.6 dynamic_slice.43
  44.1 3.1 %select_reduce_fusion.4 = f32[2,4096]{1,0:T(2,128)S(1)} fusion(pred[64,4096]{1,0:T(8,128)(4,1)S(1)} %iota_compare_fusion.14, f32[128,512]{1,0:T(8,128)S(1)} %get-tuple-element.265, s32[4096]{0:T(1024)S(1)} %bitcast.76), kind=kOutput, calls=%fused_computation.8.clone.1 | convolution fusion | flops 3224363008 | bytes 573440 | tf_op jit(solution)/shard_map/while/body/eval_jaxpr/dot_general | solution.py:69
  47.3 0.6 dynamic_slice.43
  48.7 3.1 %select_reduce_fusion.4 = f32[2,4096]{1,0:T(2,128)S(1)} fusion(pred[64,4096]{1,0:T(8,128)(4,1)S(1)} %iota_compare_fusion.14, f32[128,512]{1,0:T(8,128)S(1)} %get-tuple-element.265, s32[4096]{0:T(1024)S(1)} %bitcast.76), kind=kOutput, calls=%fused_computation.8.clone.1 | convolution fusion | flops 3224363008 | bytes 573440 | tf_op jit(solution)/shard_map/while/body/eval_jaxpr/dot_general | solution.py:69
  51.8 0.6 dynamic_slice.43
  53.2 3.1 %select_reduce_fusion.4 = f32[2,4096]{1,0:T(2,128)S(1)} fusion(pred[64,4096]{1,0:T(8,128)(4,1)S(1)} %iota_compare_fusion.14, f32[128,512]{1,0:T(8,128)S(1)} %get-tuple-element.265, s32[4096]{0:T(1024)S(1)} %bitcast.76), kind=kOutput, calls=%fused_computation.8.clone.1 | convolution fusion | flops 3224363008 | bytes 573440 | tf_op jit(solution)/shard_map/while/body/eval_jaxpr/dot_general | solution.py:69
  56.3 0.6 dynamic_slice.43
  57.8 3.1 %select_reduce_fusion.4 = f32[2,4096]{1,0:T(2,128)S(1)} fusion(pred[64,4096]{1,0:T(8,128)(4,1)S(1)} %iota_compare_fusion.14, f32[128,512]{1,0:T(8,128)S(1)} %get-tuple-element.265, s32[4096]{0:T(1024)S(1)} %bitcast.76), kind=kOutput, calls=%fused_computation.8.clone.1 | convolution fusion | flops 3224363008 | bytes 573440 | tf_op jit(solution)/shard_map/while/body/eval_jaxpr/dot_general | solution.py:69
  62.1 0.7 copy-done.1
  63.6 1.8 %copy.20 = f32[2,32,4096]{2,0,1:T(2,128)} copy(f32[2,32,4096]{2,1,0:T(8,128)S(1)} %bitcast.71) | data formatting | bytes 2097152 | tf_op jit(solution)/shard_map/reshape | solution.py:88
  65.4 6.9 %all-to-all-start = ((f32[2,32,4096]{2,0,1:T(2,128)}), f32[2,32,4096]{2,0,1:T(2,128)S(1)}, u32[]{:S(2)}, u32[]{:S(2)}) async-start(f32[2,32,4096]{2,0,1:T(2,128)} %copy.20), calls=%async_computation | async-start | bytes 2097152 | tf_op jit(solution)/shard_map/all_to_all | solution.py:89
  72.3 1.6 constant_dynamic-update-slice_fusion.1
  73.9 1.0 mul.126
  74.9 1.9 %constant_dynamic-update-slice_fusion = f32[2,8,64,514]{3,2,1,0:T(8,128)} fusion(f32[2,8,64,514]{3,2,1,0:T(8,128)} %constant_dynamic-update-slice_fusion.1, f32[2,8,64,2]{3,2,1,0:T(8,128)} %collective-permute-done.1), kind=kLoop, calls=%fused_computation.45 | loop fusion | bytes 1048576 | tf_op jit(solution)/shard_map/concatenate | solution.py:19
  76.8 3.8 %multiply_add_fusion = f32[2,8,64,514]{3,2,1,0:T(8,128)S(1)} fusion(f32[2,8,64,514]{3,2,1,0:T(8,128)} %constant_dynamic-update-slice_fusion, f32[2,8,64,2]{3,2,1,0:T(8,128)} %collective-permute-done.1, f32[2,8,64,512]{3,2,1,0:T(8,128)S(1)} %copy-done, f32[2,8,64,2]{3,2,1,0:T(8,128)} %collective-permute-done, f32[8,64]{1,0:T(8,128)S(1)} %get-tuple-element.169, ...), kind=kLoop, calls=%fused_computation.30 | loop fusion | flops 5789696 | bytes 6328320 | tf_op jit(solution)/shard_map/add | solution.py:28
  81.3 1.3 multiply_add_fusion.1
  82.9 2.6 %pad_subtract_fusion.1 = f32[2,8,64,512]{3,2,1,0:T(8,128)} fusion(f32[2,7,64,512]{3,2,1,0:T(8,128)S(1)} %fusion.17, f32[8,64]{1,0:T(8,128)S(1)} %get-tuple-element.169, f32[2,8,64,514]{3,2,1,0:T(8,128)S(1)} %pad_subtract_fusion, f32[8,64]{1,0:T(8,128)S(1)} %get-tuple-element.168), kind=kLoop, calls=%fused_computation.33 | loop fusion | flops 5242880 | bytes 10227712 | tf_op jit(solution)/shard_map/sub | solution.py:38
  85.5 13.2 %all-to-all-done = f32[2,32,4096]{2,0,1:T(2,128)S(1)} async-done(((f32[2,32,4096]{2,0,1:T(2,128)}), f32[2,32,4096]{2,0,1:T(2,128)S(1)}, u32[]{:S(2)}, u32[]{:S(2)}) %all-to-all-start) | async-done | bytes 1048608 | tf_op jit(solution)/shard_map/all_to_all | solution.py:89
  98.8 0.6 copy.21
  99.4 1.0 select_reduce_fusion.1
  101.0 73.8 %while.24 = (s32[]{:T(128)}, f32[128,512]{1,0:T(8,128)S(1)}, s32[12,4096]{1,0:T(8,128)}, f32[12,2,4096]{2,1,0:T(2,128)S(1)}, s32[12,4096]{1,0:T(8,128)}, /*index=5*/s32[]{:T(128)}, s32[]{:T(128)}) while((s32[]{:T(128)}, f32[128,512]{1,0:T(8,128)S(1)}, s32[12,4096]{1,0:T(8,128)}, f32[12,2,4096]{2,1,0:T(2,128)S(1)}, ...), condition=%wide.region_6.7_spmd.clone, body=%wide.region_5.6_spmd.clone.sunk | while | flops 3224240128 | bytes 5439583 | solution.py:121
  101.0 1.1 constant_dynamic-slice_fusion.7
  102.4 4.7 %fusion.31 = f32[128,512]{1,0:T(8,128)S(1)} fusion(f32[128,4096]{1,0:T(8,128)S(1)} %bitcast.68, s32[4096]{0:T(1024)S(1)} %bitcast.75, f32[128,512]{1,0:T(8,128)S(1)} %get-tuple-element.275, pred[]{:T(512)S(6)} %compare.17), kind=kOutput, calls=%fused_computation.18.clone.1 | convolution fusion | flops 3223453696 | bytes 2637825 | tf_op jit(solution)/shard_map/while/body/eval_jaxpr/dot_general | solution.py:111
  107.2 1.0 constant_dynamic-slice_fusion.7
  108.6 4.7 %fusion.31 = f32[128,512]{1,0:T(8,128)S(1)} fusion(f32[128,4096]{1,0:T(8,128)S(1)} %bitcast.68, s32[4096]{0:T(1024)S(1)} %bitcast.75, f32[128,512]{1,0:T(8,128)S(1)} %get-tuple-element.275, pred[]{:T(512)S(6)} %compare.17), kind=kOutput, calls=%fused_computation.18.clone.1 | convolution fusion | flops 3223453696 | bytes 2637825 | tf_op jit(solution)/shard_map/while/body/eval_jaxpr/dot_general | solution.py:111
  113.4 1.0 constant_dynamic-slice_fusion.7
  114.7 4.7 %fusion.31 = f32[128,512]{1,0:T(8,128)S(1)} fusion(f32[128,4096]{1,0:T(8,128)S(1)} %bitcast.68, s32[4096]{0:T(1024)S(1)} %bitcast.75, f32[128,512]{1,0:T(8,128)S(1)} %get-tuple-element.275, pred[]{:T(512)S(6)} %compare.17), kind=kOutput, calls=%fused_computation.18.clone.1 | convolution fusion | flops 3223453696 | bytes 2637825 | tf_op jit(solution)/shard_map/while/body/eval_jaxpr/dot_general | solution.py:111
  119.5 1.0 constant_dynamic-slice_fusion.7
  120.9 4.7 %fusion.31 = f32[128,512]{1,0:T(8,128)S(1)} fusion(f32[128,4096]{1,0:T(8,128)S(1)} %bitcast.68, s32[4096]{0:T(1024)S(1)} %bitcast.75, f32[128,512]{1,0:T(8,128)S(1)} %get-tuple-element.275, pred[]{:T(512)S(6)} %compare.17), kind=kOutput, calls=%fused_computation.18.clone.1 | convolution fusion | flops 3223453696 | bytes 2637825 | tf_op jit(solution)/shard_map/while/body/eval_jaxpr/dot_general | solution.py:111
  125.7 1.0 constant_dynamic-slice_fusion.7
  127.0 4.7 %fusion.31 = f32[128,512]{1,0:T(8,128)S(1)} fusion(f32[128,4096]{1,0:T(8,128)S(1)} %bitcast.68, s32[4096]{0:T(1024)S(1)} %bitcast.75, f32[128,512]{1,0:T(8,128)S(1)} %get-tuple-element.275, pred[]{:T(512)S(6)} %compare.17), kind=kOutput, calls=%fused_computation.18.clone.1 | convolution fusion | flops 3223453696 | bytes 2637825 | tf_op jit(solution)/shard_map/while/body/eval_jaxpr/dot_general | solution.py:111
  131.8 1.0 constant_dynamic-slice_fusion.7
  133.2 4.7 %fusion.31 = f32[128,512]{1,0:T(8,128)S(1)} fusion(f32[128,4096]{1,0:T(8,128)S(1)} %bitcast.68, s32[4096]{0:T(1024)S(1)} %bitcast.75, f32[128,512]{1,0:T(8,128)S(1)} %get-tuple-element.275, pred[]{:T(512)S(6)} %compare.17), kind=kOutput, calls=%fused_computation.18.clone.1 | convolution fusion | flops 3223453696 | bytes 2637825 | tf_op jit(solution)/shard_map/while/body/eval_jaxpr/dot_general | solution.py:111
  137.9 1.0 constant_dynamic-slice_fusion.7
  139.3 4.7 %fusion.31 = f32[128,512]{1,0:T(8,128)S(1)} fusion(f32[128,4096]{1,0:T(8,128)S(1)} %bitcast.68, s32[4096]{0:T(1024)S(1)} %bitcast.75, f32[128,512]{1,0:T(8,128)S(1)} %get-tuple-element.275, pred[]{:T(512)S(6)} %compare.17), kind=kOutput, calls=%fused_computation.18.clone.1 | convolution fusion | flops 3223453696 | bytes 2637825 | tf_op jit(solution)/shard_map/while/body/eval_jaxpr/dot_general | solution.py:111
  144.1 1.0 constant_dynamic-slice_fusion.7
  145.5 4.7 %fusion.31 = f32[128,512]{1,0:T(8,128)S(1)} fusion(f32[128,4096]{1,0:T(8,128)S(1)} %bitcast.68, s32[4096]{0:T(1024)S(1)} %bitcast.75, f32[128,512]{1,0:T(8,128)S(1)} %get-tuple-element.275, pred[]{:T(512)S(6)} %compare.17), kind=kOutput, calls=%fused_computation.18.clone.1 | convolution fusion | flops 3223453696 | bytes 2637825 | tf_op jit(solution)/shard_map/while/body/eval_jaxpr/dot_general | solution.py:111
  150.2 1.0 constant_dynamic-slice_fusion.7
  151.6 4.7 %fusion.31 = f32[128,512]{1,0:T(8,128)S(1)} fusion(f32[128,4096]{1,0:T(8,128)S(1)} %bitcast.68, s32[4096]{0:T(1024)S(1)} %bitcast.75, f32[128,512]{1,0:T(8,128)S(1)} %get-tuple-element.275, pred[]{:T(512)S(6)} %compare.17), kind=kOutput, calls=%fused_computation.18.clone.1 | convolution fusion | flops 3223453696 | bytes 2637825 | tf_op jit(solution)/shard_map/while/body/eval_jaxpr/dot_general | solution.py:111
  156.4 1.0 constant_dynamic-slice_fusion.7
  157.8 4.7 %fusion.31 = f32[128,512]{1,0:T(8,128)S(1)} fusion(f32[128,4096]{1,0:T(8,128)S(1)} %bitcast.68, s32[4096]{0:T(1024)S(1)} %bitcast.75, f32[128,512]{1,0:T(8,128)S(1)} %get-tuple-element.275, pred[]{:T(512)S(6)} %compare.17), kind=kOutput, calls=%fused_computation.18.clone.1 | convolution fusion | flops 3223453696 | bytes 2637825 | tf_op jit(solution)/shard_map/while/body/eval_jaxpr/dot_general | solution.py:111
  162.5 1.0 constant_dynamic-slice_fusion.7
  163.9 4.7 %fusion.31 = f32[128,512]{1,0:T(8,128)S(1)} fusion(f32[128,4096]{1,0:T(8,128)S(1)} %bitcast.68, s32[4096]{0:T(1024)S(1)} %bitcast.75, f32[128,512]{1,0:T(8,128)S(1)} %get-tuple-element.275, pred[]{:T(512)S(6)} %compare.17), kind=kOutput, calls=%fused_computation.18.clone.1 | convolution fusion | flops 3223453696 | bytes 2637825 | tf_op jit(solution)/shard_map/while/body/eval_jaxpr/dot_general | solution.py:111
  168.7 1.0 constant_dynamic-slice_fusion.7
  170.1 4.7 %fusion.31 = f32[128,512]{1,0:T(8,128)S(1)} fusion(f32[128,4096]{1,0:T(8,128)S(1)} %bitcast.68, s32[4096]{0:T(1024)S(1)} %bitcast.75, f32[128,512]{1,0:T(8,128)S(1)} %get-tuple-element.275, pred[]{:T(512)S(6)} %compare.17), kind=kOutput, calls=%fused_computation.18.clone.1 | convolution fusion | flops 3223453696 | bytes 2637825 | tf_op jit(solution)/shard_map/while/body/eval_jaxpr/dot_general | solution.py:111
  174.9 1.1 add_bitcast_fusion
  176.0 0.7 fusion.18
  (130 shorter events, 17.2 us)
Async XLA Ops:
  0.6 7.0 %slice-start = ((f32[2,8,64,512]{3,2,1,0:T(8,128)}), f32[2,1,64,512]{3,2,1,0:T(8,128)S(1)}, s32[]{:S(2)}) async-start(f32[2,8,64,512]{3,2,1,0:T(8,128)} %param.15), calls=%async_computation.1 | async-start | bytes 524288 | tf_op jit(solution)/shard_map/slice | solution.py:58
  0.6 6.7 %copy-start.5 = (s32[1,1,3,4,4096]{4,3,2,1,0:T(4,128)S(1)}, s32[1,1,3,4,4096]{4,3,2,1,0:T(4,128)}, u32[]{:S(2)}) copy-start(s32[1,1,3,4,4096]{4,3,2,1,0:T(4,128)} %param.21) | copy-start | bytes 589828
  0.7 6.7 %copy-start.6 = (s32[1,1,3,4,4096]{4,3,2,1,0:T(4,128)S(1)}, s32[1,1,3,4,4096]{4,3,2,1,0:T(4,128)}, u32[]{:S(2)}) copy-start(s32[1,1,3,4,4096]{4,3,2,1,0:T(4,128)} %param.22) | copy-start | bytes 589828
  0.7 6.8 %copy-start.11 = (s32[1,1,3,4]{3,1,2,0:T(1,128)S(1)}, s32[1,1,3,4]{3,1,2,0:T(1,128)}, u32[]{:S(2)}) copy-start(s32[1,1,3,4]{3,1,2,0:T(1,128)} %param.20) | copy-start | bytes 148
  3.1 71.8 %collective-permute-start.1 = (f32[2,8,64,2]{3,2,1,0:T(8,128)}, f32[2,8,64,2]{3,2,1,0:T(8,128)}, u32[]{:S(2)}, u32[]{:S(2)}) collective-permute-start(f32[2,8,64,2]{3,2,1,0:T(8,128)} %get-tuple-element.167), channel_id=1, source_target_pairs={{1,0},{2,1},{3,2},{4,3},{5,4},{6,5},{7,6},{0,7},{9,8},{10,9},{11,1... | collective-permute-start | bytes 24584 | tf_op jit(solution)/shard_map/ppermute | solution.py:18
  7.3 69.5 %collective-permute-start = (f32[2,8,64,2]{3,2,1,0:T(8,128)}, f32[2,8,64,2]{3,2,1,0:T(8,128)}, u32[]{:S(2)}, u32[]{:S(2)}) collective-permute-start(f32[2,8,64,2]{3,2,1,0:T(8,128)} %get-tuple-element.166), channel_id=1, source_target_pairs={{0,1},{1,2},{2,3},{3,4},{4,5},{5,6},{6,7},{7,0},{8,9},{9,10},{10,1... | collective-permute-start | bytes 24584 | tf_op jit(solution)/shard_map/ppermute | solution.py:15
  62.1 0.7 copy-start.1
  62.1 1.4 copy-start.2
  63.5 8.7 %copy-start.10 = (f32[8,64]{1,0:T(8,128)S(1)}, f32[8,64]{1,0:T(8,128)}, u32[]{:S(2)}) copy-start(f32[8,64]{1,0:T(8,128)} %param.16) | copy-start | bytes 6148
  63.5 8.7 %copy-start = (f32[2,8,64,512]{3,2,1,0:T(8,128)S(1)}, f32[2,8,64,512]{3,2,1,0:T(8,128)}, u32[]{:S(2)}) copy-start(f32[2,8,64,512]{3,2,1,0:T(8,128)} %param.15) | copy-start | bytes 6291460
  65.4 33.4 %all-to-all-start = ((f32[2,32,4096]{2,0,1:T(2,128)}), f32[2,32,4096]{2,0,1:T(2,128)S(1)}, u32[]{:S(2)}, u32[]{:S(2)}) async-start(f32[2,32,4096]{2,0,1:T(2,128)} %copy.20), calls=%async_computation | async-start | bytes 2097152 | tf_op jit(solution)/shard_map/all_to_all | solution.py:89
  76.8 3.8 %copy-start.9 = (f32[7,64]{1,0:T(8,128)S(1)}, f32[7,64]{1,0:T(8,128)}, u32[]{:S(2)}) copy-start(f32[7,64]{1,0:T(8,128)} %param.17) | copy-start | bytes 5380
  99.4 1.6 copy-start.3
  101.0 73.9 %copy-start.7 = (f32[64,512]{1,0:T(8,128)S(1)}, f32[64,512]{1,0:T(8,128)}, u32[]{:S(2)}) copy-start(f32[64,512]{1,0:T(8,128)} %param.18) | copy-start | bytes 393220
  101.0 73.9 %copy-start.8 = (s32[64,512]{1,0:T(8,128)S(1)}, s32[64,512]{1,0:T(8,128)}, u32[]{:S(2)}) copy-start(s32[64,512]{1,0:T(8,128)} %param.19) | copy-start | bytes 393220
  174.8 1.9 %copy-start.4 = (f32[128,512]{1,0:T(8,128)}, f32[128,512]{1,0:T(8,128)S(1)}, u32[]{:S(2)}) copy-start(f32[128,512]{1,0:T(8,128)S(1)} %get-tuple-element.99) | copy-start | bytes 786436
where the time goes:
time: 179 us; the launch traced here: 177 us
  matrix products  94.5 us (53%)
  local copies, waits for them, and re-layouts  30.5 us (17%)
  other arithmetic  25.3 us (14%)
  waiting for transfers between devices  13.2 us (7%)
  starting transfers between devices  11.1 us (6%)
    dot_general x12, matrix products, land_list(): lax.dot_general(spread, col_table, (((1,), (1,)), ((), ())), precision=la...  56.9 us
    dot_general x12, matrix products, pick_list(): jnp.dot(surface_rows, col_table, precision=lax.Precision.HIGHEST, preferr...  37.6 us
    dynamic_slice x36, local copies, waits for them, and re-layouts, shards(): unused, picked_all = lax.scan(pick_list, 0, (row_lists, col_lists, counts))  19.5 us
    all_to_all x1, waiting for transfers between devices, shards(): lax.all_to_all(blocks, ('comp', 'tile'), split_axis=1, concat_axis=1, til...  13.2 us
    all_to_all x1, starting transfers between devices, shards(): lax.all_to_all(blocks, ('comp', 'tile'), split_axis=1, concat_axis=1, til...  6.86 us
    lt x12, other arithmetic, pick_list(): values = jnp.where((slot_iota < count_one)[None, :], values, 0.0)  6.79 us
    add x2, other arithmetic, transport(): middle - 0.5 * speed * (right - left)  5.15 us
    ppermute x1, starting transfers between devices, with_halo(): lax.ppermute(lax.slice_in_dim(block, 0, width, axis=dim), axis, backward)  4.25 us
  transfers between devices with their start and end apart: 3, of which 1 were waited for; matrix products, arithmetic and copies ran while one was open for 40% of the time, Pallas kernels for 0%

commit v1 on v0

v1 whole, which is shorter than its diff:
```python
import functools

import jax
import jax.numpy as jnp
from jax import lax
from jax.experimental import pallas as pl
from jax.experimental.pallas import tpu as pltpu
from jax.sharding import PartitionSpec as P

SUBSTEPS = 2
LANES = 128
MESH = pl.DeviceIdType.MESH
SHIFT = 256


def chunk_of(slot_count):
    for width in (1024, 512, 256):
        if slot_count % width == 0:
            return width
    return slot_count


def one_hot(iota_ref, key, depth):
    width = key.shape[1]
    shifted = (key - SHIFT).astype(jnp.float32)
    wide = jnp.broadcast_to(shifted, (16, width)).astype(jnp.bfloat16)
    one = jnp.ones((16, width), jnp.bfloat16)
    zero = jnp.zeros((16, width), jnp.bfloat16)
    parts = []
    for start in range(0, depth, 16):
        number = iota_ref[start : start + 16, :]
        number = jnp.concatenate([number] * (width // LANES), axis=1)
        parts.append(jnp.where(wide == number, one, zero))
    return jnp.concatenate(parts, axis=0)


def split(values):
    high = values.astype(jnp.bfloat16)
    low = (values - high.astype(jnp.float32)).astype(jnp.bfloat16)
    return high, low


def keys_of(which, row, col, row_count, col_count):
    if which == 1:
        return col, row
    half = row_count // 2
    edge = col_count // 4
    base = 0 if which == 0 else col_count - edge
    upper = (row >= half).astype(jnp.int32)
    return upper * edge + (col - base), row - upper * half


def exchange_kernel(
    row_count,
    col_count,
    slot_count,
    comp_total,
    tile_total,
    fl_count,
    state_ref,
    count_ref,
    row_ref,
    col_ref,
    weight_ref,
    partner_ref,
    halo_ref,
    surface,
    edges,
    table_mid,
    table_side,
    outgoing,
    incoming,
    halo_out,
    halo_in,
    total_mid,
    total_side,
    iota_ref,
    load_sem,
    send_sem,
    recv_sem,
    halo_send_sem,
    halo_recv_sem,
):
    comp = lax.axis_index("comp")
    tile = lax.axis_index("tile")
    ocean = comp == comp_total - 1
    tiles = [lax.rem(tile + offset + tile_total, tile_total) for offset in (-1, 0, 1)]
    fields = surface.shape[0]
    half = row_count // 2
    edge = col_count // 4
    width = chunk_of(slot_count)
    chunks = slot_count // width
    low_list = jnp.where(ocean, 0, comp_total - 1)
    high_list = jnp.where(ocean, comp_total - 1, comp_total)

    load_surface = pltpu.make_async_copy(state_ref.at[:, 0], surface, load_sem.at[0])
    load_surface.start()
    loads = []
    for side, start in ((0, 0), (1, col_count - LANES)):
        load = pltpu.make_async_copy(
            state_ref.at[:, :, :, pl.ds(start, LANES)], edges.at[side], load_sem.at[1 + side]
        )
        load.start()
        loads.append(load)

    barrier = pltpu.get_barrier_semaphore()
    for which in (0, 2):
        pl.semaphore_signal(barrier, inc=1, device_id=(comp, tiles[which]), device_id_type=MESH)

    def greet(other, carry):
        for which in range(3):
            pl.semaphore_signal(
                barrier, inc=1, device_id=(other, tiles[which]), device_id_type=MESH
            )
        return carry

    lax.fori_loop(low_list, high_list, greet, 0)

    iota_ref[...] = (lax.broadcasted_iota(jnp.int32, iota_ref.shape, 0) - SHIFT).astype(
        jnp.float32
    ).astype(jnp.bfloat16)
    load_surface.wait()
    for field in range(fields):
        value = surface[field]
        high, low = split(value)
        for index, piece in ((field, high), (fields + field, low)):
            table_mid[index * row_count : (index + 1) * row_count, :] = piece
            for side, base in ((0, 0), (1, col_count - edge)):
                table_side[side, index * half : (index + 1) * half, :] = jnp.concatenate(
                    [piece[:half, base : base + edge], piece[half:, base : base + edge]], axis=1
                )
    total_mid[...] = jnp.zeros_like(total_mid)
    total_side[...] = jnp.zeros_like(total_side)

    pl.semaphore_wait(barrier, 2 + 3 * (high_list - low_list))

    def copy_of(which, other):
        return pltpu.make_async_remote_copy(
            src_ref=outgoing.at[which, other],
            dst_ref=incoming.at[2 - which, comp],
            send_sem=send_sem.at[which, other],
            recv_sem=recv_sem.at[2 - which, comp],
            device_id=(other, tiles[which]),
            device_id_type=MESH,
        )

    def landing_of(which, other):
        return pltpu.make_async_remote_copy(
            src_ref=outgoing.at[which, other],
            dst_ref=incoming.at[which, other],
            send_sem=send_sem.at[which, other],
            recv_sem=recv_sem.at[which, other],
            device_id=(other, tiles[which]),
            device_id_type=MESH,
        )

    def pick(other, carry):
        for which in (1, 0, 2):
            count = count_ref[which, other]

            def pick_chunk(piece, inner):
                start = pl.multiple_of(piece * width, width)
                span = pl.ds(start, width)
                row = row_ref[which, pl.ds(other, 1), span]
                col = col_ref[which, pl.ds(other, 1), span]
                key, inside = keys_of(which, row, col, row_count, col_count)
                if which == 1:
                    table, depth, rows = table_mid[...], col_count, row_count
                else:
                    table, depth, rows = table_side[which // 2], 2 * edge, half
                picked = jnp.dot(
                    table, one_hot(iota_ref, key, depth), preferred_element_type=jnp.float32
                )
                match = lax.broadcasted_iota(jnp.int32, (rows, width), 0) == inside
                live = lax.broadcasted_iota(jnp.int32, (1, width), 1) + start < count
                for field in range(fields):
                    both = (
                        picked[field * rows : (field + 1) * rows]
                        + picked[(fields + field) * rows : (fields + field + 1) * rows]
                    )
                    value = jnp.sum(jnp.where(match, both, 0.0), axis=0, keepdims=True)
                    outgoing[which, other, field : field + 1, span] = jnp.where(live, value, 0.0)
                return inner

            lax.fori_loop(0, chunks, pick_chunk, 0)
            copy_of(which, other).start()
        return carry

    lax.fori_loop(low_list, high_list, pick, 0)

    for load in loads:
        load.wait()
    lane = lax.broadcasted_iota(jnp.int32, (row_count, LANES), 1)
    for side in range(2):
        packed = jnp.zeros((row_count, LANES), jnp.float32)
        for place in range(fl_count):
            level = edges[side, place // (fl_count // fields), place % (fl_count // fields)]
            shift = SUBSTEPS * place + (0 if side == 0 else SUBSTEPS)
            moved = level if shift == 0 else pltpu.roll(level, shift, 1)
            packed = jnp.where(lane // SUBSTEPS == place, moved, packed)
        halo_out[side] = packed

    def halo_copy(side):
        return pltpu.make_async_remote_copy(
            src_ref=halo_out.at[side],
            dst_ref=halo_in.at[1 - side],
            send_sem=halo_send_sem.at[side],
            recv_sem=halo_recv_sem.at[1 - side],
            device_id=(comp, tiles[2 * side]),
            device_id_type=MESH,
        )

    for side in range(2):
        halo_copy(side).start()

    def land(other, carry):
        for which in (1, 0, 2):
            landing_of(which, other).wait_recv()

            def land_chunk(piece, inner):
                start = pl.multiple_of(piece * width, width)
                span = pl.ds(start, width)
                row = row_ref[which, pl.ds(other, 1), span]
                col = col_ref[which, pl.ds(other, 1), span]
                key, inside = keys_of(which, row, col, row_count, col_count)
                depth, rows = (
                    (col_count, row_count) if which == 1 else (2 * edge, half)
                )
                term = incoming[which, other, :, span] * weight_ref[which, pl.ds(other, 1), span]
                high, low = split(term)
                wide_key = jnp.broadcast_to(
                    inside.astype(jnp.float32) - SHIFT, (16, width)
                ).astype(jnp.bfloat16)
                zero = jnp.zeros((16, width), jnp.bfloat16)
                parts = []
                matches = []
                for first in range(0, rows, 16):
                    number = iota_ref[first : first + 16, :]
                    number = jnp.concatenate([number] * (width // LANES), axis=1)
                    matches.append(wide_key == number)
                for piece_of in (high, low):
                    for field in range(fields):
                        value = jnp.broadcast_to(
                            piece_of[field : field + 1].astype(jnp.float32), (16, width)
                        ).astype(jnp.bfloat16)
                        for match in matches:
                            parts.append(jnp.where(match, value, zero))
                spread = jnp.concatenate(parts, axis=0)
                added = lax.dot_general(
                    spread,
                    one_hot(iota_ref, key, depth),
                    (((1,), (1,)), ((), ())),
                    preferred_element_type=jnp.float32,
                )
                if which == 1:
                    total_mid[...] += added
                else:
                    total_side[which // 2] += added
                return inner

            lax.fori_loop(0, chunks, land_chunk, 0)
        return carry

    lax.fori_loop(low_list, high_list, land, 0)

    for field in range(fields):
        first, second = field, fields + field
        whole = (
            total_mid[first * row_count : (first + 1) * row_count, :]
            + total_mid[second * row_count : (second + 1) * row_count, :]
        )
        partner_ref[field] = whole
        for side, base in ((0, 0), (1, col_count - edge)):
            extra = (
                total_side[side, first * half : (first + 1) * half, :]
                + total_side[side, second * half : (second + 1) * half, :]
            )
            partner_ref[field, :half, base : base + edge] += extra[:, :edge]
            partner_ref[field, half:, base : base + edge] += extra[:, edge:]

    def finish(other, carry):
        for which in range(3):
            copy_of(which, other).wait_send()
        return carry

    lax.fori_loop(low_list, high_list, finish, 0)
    for side in range(2):
        copy = halo_copy(side)
        copy.wait_send()
    for side in range(2):
        halo_copy(1 - side).wait_recv()
        halo_ref[side] = halo_in[side]


def advance_kernel(
    state_ref,
    courant_ref,
    mixing_ref,
    exchange_ref,
    sea_ref,
    halo_ref,
    partner_in_ref,
    new_ref,
    partner_ref,
    speed_ref,
    mix_ref,
):
    fields, levels, rows, cols = state_ref.shape
    step = pl.program_id(0)
    ocean = lax.axis_index("comp") == lax.axis_size("comp") - 1

    @pl.when(step == 0)
    def _():
        speed_ref[...] = jnp.transpose(courant_ref[...])
        mix_ref[...] = jnp.transpose(mixing_ref[...])

    span = pl.ds(pl.multiple_of(step * rows, rows), rows)
    total = cols + LANES
    lane = lax.broadcasted_iota(jnp.int32, (rows, LANES), 1)
    speeds = speed_ref[span, :]
    mixes = mix_ref[span, :]
    surface = []
    for field in range(fields):
        columns = []
        for level in range(levels):
            place = field * levels + level
            east = halo_ref[1]
            east = east if place == 0 else pltpu.roll(east, LANES - SUBSTEPS * place, 1)
            west = pltpu.roll(halo_ref[0], LANES - SUBSTEPS * (place + 1), 1)
            ends = jnp.where(lane < LANES // 2, east, west)
            columns.append(jnp.concatenate([state_ref[field, level], ends], axis=1))
        for substep in range(SUBSTEPS):
            moved = []
            for level in range(levels):
                c = jnp.broadcast_to(speeds[:, level : level + 1], (rows, total))
                q = columns[level]
                left = pltpu.roll(q, 1, 1)
                right = pltpu.roll(q, total - 1, 1)
                moved.append(q - 0.5 * c * (right - left) + 0.5 * c * c * (right - 2.0 * q + left))
            columns = []
            flux = None
            for level in range(levels):
                value = moved[level]
                if level < levels - 1:
                    m = jnp.broadcast_to(mixes[:, level : level + 1], (rows, total))
                    above = m * (moved[level + 1] - moved[level])
                    value = value + above
                if level > 0:
                    value = value - flux
                if level < levels - 1:
                    flux = above
                columns.append(value)
        for level in range(1, levels):
            new_ref[field, level] = columns[level][:, :cols]
        surface.append(columns[0][:, :cols])
    rate = exchange_ref[...] * sea_ref[...].astype(jnp.float32)
    first, second = surface
    far = partner_in_ref[0]
    far_second = partner_in_ref[1]
    new_ref[0, 0] = first + rate * (far - first)
    air = second + rate * (1.2 * far - 0.3 * far_second - second)
    sea = second + rate * (1.2 * first - far_second)
    new_ref[1, 0] = jnp.where(ocean, sea, air)
    partner_ref[...] = partner_in_ref[...]


def shards(
    state,
    courant,
    mixing,
    exchange_coef,
    sea_mask,
    margin_count,
    margin_row,
    margin_col,
    margin_weight,
):
    fields, levels, rows, cols = state.shape
    slots = margin_row.shape[-1]
    comp_total = lax.axis_size("comp")
    tile_total = lax.axis_size("tile")
    half = rows // 2
    edge = cols // 4
    lists = (3, comp_total, slots)
    vmem = pl.BlockSpec(memory_space=pltpu.VMEM)
    partner, halo = pl.pallas_call(
        functools.partial(
            exchange_kernel, rows, cols, slots, comp_total, tile_total, fields * levels
        ),
        out_shape=(
            jax.ShapeDtypeStruct((fields, rows, cols), jnp.float32),
            jax.ShapeDtypeStruct((2, rows, LANES), jnp.float32),
        ),
        in_specs=[
            pl.BlockSpec(memory_space=pl.ANY),
            pl.BlockSpec(memory_space=pltpu.SMEM),
            vmem,
            vmem,
            vmem,
        ],
        out_specs=(vmem, vmem),
        scratch_shapes=[
            pltpu.VMEM((fields, rows, cols), jnp.float32),
            pltpu.VMEM((2, fields, levels, rows, LANES), jnp.float32),
            pltpu.VMEM((2 * fields * rows, cols), jnp.bfloat16),
            pltpu.VMEM((2, 2 * fields * half, 2 * edge), jnp.bfloat16),
            pltpu.VMEM((3, comp_total, fields, slots), jnp.float32),
            pltpu.VMEM((3, comp_total, fields, slots), jnp.float32),
            pltpu.VMEM((2, rows, LANES), jnp.float32),
            pltpu.VMEM((2, rows, LANES), jnp.float32),
            pltpu.VMEM((2 * fields * rows, cols), jnp.float32),
            pltpu.VMEM((2, 2 * fields * half, 2 * edge), jnp.float32),
            pltpu.VMEM((cols, LANES), jnp.bfloat16),
            pltpu.SemaphoreType.DMA((3,)),
            pltpu.SemaphoreType.DMA((3, comp_total)),
            pltpu.SemaphoreType.DMA((3, comp_total)),
            pltpu.SemaphoreType.DMA((2,)),
            pltpu.SemaphoreType.DMA((2,)),
        ],
        compiler_params=pltpu.CompilerParams(
            collective_id=0, has_side_effects=True, vmem_limit_bytes=48 * 1024 * 1024
        ),
    )(
        state,
        margin_count.reshape(3, comp_total),
        margin_row.reshape(lists),
        margin_col.reshape(lists),
        margin_weight.reshape(lists),
    )
    block = 8
    plane = pl.BlockSpec((block, cols), lambda i: (i, 0))
    return pl.pallas_call(
        advance_kernel,
        grid=(rows // block,),
        out_shape=(
            jax.ShapeDtypeStruct(state.shape, jnp.float32),
            jax.ShapeDtypeStruct((fields, rows, cols), jnp.float32),
        ),
        in_specs=[
            pl.BlockSpec((fields, levels, block, cols), lambda i: (0, 0, i, 0)),
            pl.BlockSpec(courant.shape, lambda i: (0, 0)),
            pl.BlockSpec(mixing.shape, lambda i: (0, 0)),
            plane,
            plane,
            pl.BlockSpec((2, block, LANES), lambda i: (0, i, 0)),
            pl.BlockSpec((fields, block, cols), lambda i: (0, i, 0)),
        ],
        out_specs=(
            pl.BlockSpec((fields, levels, block, cols), lambda i: (0, 0, i, 0)),
            pl.BlockSpec((fields, block, cols), lambda i: (0, i, 0)),
        ),
        scratch_shapes=[
            pltpu.VMEM((rows, levels), jnp.float32),
            pltpu.VMEM((rows, levels - 1), jnp.float32),
        ],
    )(state, courant, mixing, exchange_coef, sea_mask, halo, partner)


def solution(mesh):
    in_specs = (
        P(None, None, "comp", "tile"),
        P(None, "comp"),
        P(None, "comp"),
        P("comp", "tile"),
        P("comp", "tile"),
        P("comp", "tile", None, None),
        P("comp", "tile", None, None, None),
        P("comp", "tile", None, None, None),
        P("comp", "tile", None, None, None),
    )
    out_specs = (P(None, None, "comp", "tile"), P(None, "comp", "tile"))
    return jax.shard_map(shards, mesh=mesh, in_specs=in_specs, out_specs=out_specs, check_vma=False)
```

time: 179 us -> 47.3 us (0.26); the launches traced: 177 us -> 46.9 us
  matrix products: 94.5 us -> 0 us
  Pallas kernels: 0 us -> 39.9 us
  other arithmetic: 25.3 us -> 0 us
  local copies, waits for them, and re-layouts: 30.5 us -> 6.37 us
  waiting for transfers between devices: 13.2 us -> 0 us
  starting transfers between devices: 11.1 us -> 0 us
    dot_general x24 -> x0, matrix products: 94.5 us -> none  [the longest x12 56.9 us: land_list(): lax.dot_general(spread, col_table, (((1,), (1,)), ((), ())), precision=la...]
    pallas_call x0 -> x2, Pallas kernels: none -> 39.9 us  [the longest x1 31.7 us: shards(): pl.pallas_call(functools.partial(exchange_kernel, rows, cols, slots, comp...]
    dynamic_slice x36 -> x0, local copies, waits for them, and re-layouts: 19.5 us -> none  [shards(): unused, picked_all = lax.scan(pick_list, 0, (row_lists, col_lists, counts))]
    all_to_all x1 -> x0, waiting for transfers between devices: 13.2 us -> none  [shards(): lax.all_to_all(blocks, ('comp', 'tile'), split_axis=1, concat_axis=1, til...]
    all_to_all x1 -> x0, starting transfers between devices: 6.86 us -> none  [shards(): lax.all_to_all(blocks, ('comp', 'tile'), split_axis=1, concat_axis=1, til...]
    lt x12 -> x0, other arithmetic: 6.79 us -> none  [pick_list(): values = jnp.where((slot_iota < count_one)[None, :], values, 0.0)]
    add x2 -> x0, other arithmetic: 5.15 us -> none  [transport(): middle - 0.5 * speed * (right - left)]
    ppermute x2 -> x0, starting transfers between devices: 4.25 us -> none  [the longest x1 4.25 us: with_halo(): lax.ppermute(lax.slice_in_dim(block, 0, width, axis=dim), axis, backward)]
  transfers between devices with their start and end apart: 3 -> 0, of which waited for: 1 -> 0; matrix products, arithmetic and copies ran while one was open for 40% -> 0% of each run, Pallas kernels for 0% -> 0%
where the time goes in v1:
time: 47.3 us; the launch traced here: 46.9 us
  Pallas kernels  39.9 us (84%)
  local copies, waits for them, and re-layouts  6.37 us (13%)
  between operations  0.65 us (1%)
    pallas_call x1, Pallas kernels, shards(): pl.pallas_call(functools.partial(exchange_kernel, rows, cols, slots, comp...  31.7 us
    pallas_call x1, Pallas kernels, shards(): pl.pallas_call(advance_kernel, grid=(rows // block,), out_shape=(jax.Shap...  8.23 us
    unnamed x13, local copies, waits for them, and re-layouts  6.37 us

profile of v1, /device:TPU:5, one launch (start us, length us, event | category | flops | bytes accessed | tf_op | source)
XLA Modules:
  0.0 46.9 jit_solution(7616672300546619220)
XLA Ops:
  0.6 0.7 %copy.13 = s32[1,1,3,4]{3,2,1,0:T(4,128)S(1)} copy(s32[1,1,3,4]{3,1,2,0:T(1,128)} %param.14) | data formatting | bytes 96
  1.3 0.0 copy-start
  1.3 1.6 %copy-done = f32[2,8,64,512]{3,2,1,0:T(8,128)S(1)} copy-done((f32[2,8,64,512]{3,2,1,0:T(8,128)S(1)}, f32[2,8,64,512]{3,2,1,0:T(8,128)}, u32[]{:S(2)}) %copy-start) | copy-done | bytes 2097176
  2.9 0.0 copy-start.2
  2.9 0.9 %copy-done.2 = s32[1,1,3,4,4096]{4,3,2,1,0:T(4,128)S(1)} copy-done((s32[1,1,3,4,4096]{4,3,2,1,0:T(4,128)S(1)}, s32[1,1,3,4,4096]{4,3,2,1,0:T(4,128)}, u32[]{:S(2)}) %copy-start.2) | copy-done | bytes 196632
  3.8 0.0 copy-start.3
  3.8 0.9 %copy-done.3 = s32[1,1,3,4,4096]{4,3,2,1,0:T(4,128)S(1)} copy-done((s32[1,1,3,4,4096]{4,3,2,1,0:T(4,128)S(1)}, s32[1,1,3,4,4096]{4,3,2,1,0:T(4,128)}, u32[]{:S(2)}) %copy-start.3) | copy-done | bytes 196632
  4.8 0.0 copy-start.4
  4.8 0.9 %copy-done.4 = f32[1,1,3,4,4096]{4,3,2,1,0:T(4,128)S(1)} copy-done((f32[1,1,3,4,4096]{4,3,2,1,0:T(4,128)S(1)}, f32[1,1,3,4,4096]{4,3,2,1,0:T(4,128)}, u32[]{:S(2)}) %copy-start.4) | copy-done | bytes 196632
  5.7 31.7 %shard_map.104 = (f32[2,64,512]{2,1,0:T(8,128)S(1)}, f32[2,64,128]{2,1,0:T(8,128)S(1)}) custom-call(f32[2,8,64,512]{3,2,1,0:T(8,128)S(1)} %copy-done, s32[3,4]{1,0:T(4,128)S(1)} %bitcast.9, s32[3,4,4096]{2,1,0:T(4,128)S(1)} %bitcast.6, s32[3,4,4096]{2,1,0:T(4,128)S(1)} %bitcast.7, f32[3,4,4096]{2,1,0:T(4,128)S(1)} %bitcast.8), custom_call_target="tpu_custom_call" | custom-call | tf_op jit(solution)/shard_map/pallas_call | solution.py:386
  37.4 0.0 copy-start.1
  37.4 0.7 %copy-done.1 = f32[2,64,512]{2,1,0:T(8,128)} copy-done((f32[2,64,512]{2,1,0:T(8,128)}, f32[2,64,512]{2,1,0:T(8,128)S(1)}, u32[]{:S(2)}) %copy-start.1) | copy-done | bytes 262168
  38.1 0.0 copy-start.5
  38.1 0.6 %copy-done.5 = f32[2,64,128]{2,1,0:T(8,128)} copy-done((f32[2,64,128]{2,1,0:T(8,128)}, f32[2,64,128]{2,1,0:T(8,128)S(1)}, u32[]{:S(2)}) %copy-start.5) | copy-done | bytes 65560
  38.7 8.2 %shard_map.105 = (f32[2,8,64,512]{3,2,1,0:T(8,128)}, f32[2,64,512]{2,1,0:T(8,128)}) custom-call(f32[2,8,64,512]{3,2,1,0:T(8,128)} %state_ref.3, f32[8,64]{1,0:T(8,128)} %courant_ref.1, f32[7,64]{1,0:T(8,128)} %mixing_ref.1, f32[64,512]{1,0:T(8,128)} %exchange_ref.1, s32[64,512]{1,0:T(8,128)} %sea_ref.1, f32[2,64,128]{2,1,0:T(8,128)} %copy-done.5, ...), custom_call_target="tpu_custom_call" | custom-call | tf_op jit(solution)/shard_map/pallas_call | solution.py:432
Async XLA Ops:
  1.3 1.6 %copy-start = (f32[2,8,64,512]{3,2,1,0:T(8,128)S(1)}, f32[2,8,64,512]{3,2,1,0:T(8,128)}, u32[]{:S(2)}) copy-start(f32[2,8,64,512]{3,2,1,0:T(8,128)} %state_ref.3) | copy-start | bytes 6291460
  2.9 0.9 %copy-start.2 = (s32[1,1,3,4,4096]{4,3,2,1,0:T(4,128)S(1)}, s32[1,1,3,4,4096]{4,3,2,1,0:T(4,128)}, u32[]{:S(2)}) copy-start(s32[1,1,3,4,4096]{4,3,2,1,0:T(4,128)} %param.15) | copy-start | bytes 589828
  3.8 0.9 %copy-start.3 = (s32[1,1,3,4,4096]{4,3,2,1,0:T(4,128)S(1)}, s32[1,1,3,4,4096]{4,3,2,1,0:T(4,128)}, u32[]{:S(2)}) copy-start(s32[1,1,3,4,4096]{4,3,2,1,0:T(4,128)} %param.16) | copy-start | bytes 589828
  4.8 0.9 %copy-start.4 = (f32[1,1,3,4,4096]{4,3,2,1,0:T(4,128)S(1)}, f32[1,1,3,4,4096]{4,3,2,1,0:T(4,128)}, u32[]{:S(2)}) copy-start(f32[1,1,3,4,4096]{4,3,2,1,0:T(4,128)} %param.17) | copy-start | bytes 589828
  37.4 0.7 %copy-start.1 = (f32[2,64,512]{2,1,0:T(8,128)}, f32[2,64,512]{2,1,0:T(8,128)S(1)}, u32[]{:S(2)}) copy-start(f32[2,64,512]{2,1,0:T(8,128)S(1)} %get-tuple-element.5.partner_in_ref) | copy-start | bytes 786436
  38.1 0.6 %copy-start.5 = (f32[2,64,128]{2,1,0:T(8,128)}, f32[2,64,128]{2,1,0:T(8,128)S(1)}, u32[]{:S(2)}) copy-start(f32[2,64,128]{2,1,0:T(8,128)S(1)} %get-tuple-element.4.halo_ref) | copy-start | bytes 196612

commit v2 on v1

--- a/solution.py
+++ b/solution.py
@@ -11,6 +11,7 @@
 LANES = 128
 MESH = pl.DeviceIdType.MESH
 SHIFT = 256
+VMEM_BYTES = 67043328
 
 
 def chunk_of(slot_count):
@@ -59,11 +60,15 @@
     fl_count,
     state_ref,
     count_ref,
+    row_hbm,
+    col_hbm,
+    weight_hbm,
+    partner_hbm,
+    halo_ref,
     row_ref,
     col_ref,
     weight_ref,
     partner_ref,
-    halo_ref,
     surface,
     edges,
     table_mid,
@@ -71,7 +76,6 @@
     outgoing,
     incoming,
     halo_out,
-    halo_in,
     total_mid,
     total_side,
     iota_ref,
@@ -95,6 +99,13 @@
 
     load_surface = pltpu.make_async_copy(state_ref.at[:, 0], surface, load_sem.at[0])
     load_surface.start()
+    list_loads = []
+    for place, (source, target) in enumerate(
+        ((row_hbm, row_ref), (col_hbm, col_ref), (weight_hbm, weight_ref))
+    ):
+        load = pltpu.make_async_copy(source, target, load_sem.at[3 + place])
+        load.start()
+        list_loads.append(load)
     loads = []
     for side, start in ((0, 0), (1, col_count - LANES)):
         load = pltpu.make_async_copy(
@@ -132,6 +143,8 @@
     total_mid[...] = jnp.zeros_like(total_mid)
     total_side[...] = jnp.zeros_like(total_side)
 
+    for load in list_loads:
+        load.wait()
     pl.semaphore_wait(barrier, 2 + 3 * (high_list - low_list))
 
     def copy_of(which, other):
@@ -155,12 +168,11 @@
         )
 
     def pick(other, carry):
-        for which in (1, 0, 2):
-            count = count_ref[which, other]
-
-            def pick_chunk(piece, inner):
-                start = pl.multiple_of(piece * width, width)
-                span = pl.ds(start, width)
+        def pick_chunk(piece, inner):
+            start = pl.multiple_of(piece * width, width)
+            span = pl.ds(start, width)
+            live_slot = lax.broadcasted_iota(jnp.int32, (1, width), 1) + start
+            for which in (1, 0, 2):
                 row = row_ref[which, pl.ds(other, 1), span]
                 col = col_ref[which, pl.ds(other, 1), span]
                 key, inside = keys_of(which, row, col, row_count, col_count)
@@ -172,7 +184,7 @@
                     table, one_hot(iota_ref, key, depth), preferred_element_type=jnp.float32
                 )
                 match = lax.broadcasted_iota(jnp.int32, (rows, width), 0) == inside
-                live = lax.broadcasted_iota(jnp.int32, (1, width), 1) + start < count
+                live = live_slot < count_ref[which, 0, other]
                 for field in range(fields):
                     both = (
                         picked[field * rows : (field + 1) * rows]
@@ -180,9 +192,10 @@
                     )
                     value = jnp.sum(jnp.where(match, both, 0.0), axis=0, keepdims=True)
                     outgoing[which, other, field : field + 1, span] = jnp.where(live, value, 0.0)
-                return inner
-
-            lax.fori_loop(0, chunks, pick_chunk, 0)
+            return inner
+
+        lax.fori_loop(0, chunks, pick_chunk, 0)
+        for which in range(3):
             copy_of(which, other).start()
         return carry
 
@@ -203,7 +216,7 @@
     def halo_copy(side):
         return pltpu.make_async_remote_copy(
             src_ref=halo_out.at[side],
-            dst_ref=halo_in.at[1 - side],
+            dst_ref=halo_ref.at[1 - side],
             send_sem=halo_send_sem.at[side],
             recv_sem=halo_recv_sem.at[1 - side],
             device_id=(comp, tiles[2 * side]),
@@ -214,18 +227,17 @@
         halo_copy(side).start()
 
     def land(other, carry):
-        for which in (1, 0, 2):
+        for which in range(3):
             landing_of(which, other).wait_recv()
 
-            def land_chunk(piece, inner):
-                start = pl.multiple_of(piece * width, width)
-                span = pl.ds(start, width)
+        def land_chunk(piece, inner):
+            start = pl.multiple_of(piece * width, width)
+            span = pl.ds(start, width)
+            for which in (1, 0, 2):
                 row = row_ref[which, pl.ds(other, 1), span]
                 col = col_ref[which, pl.ds(other, 1), span]
                 key, inside = keys_of(which, row, col, row_count, col_count)
-                depth, rows = (
-                    (col_count, row_count) if which == 1 else (2 * edge, half)
-                )
+                depth, rows = (col_count, row_count) if which == 1 else (2 * edge, half)
                 term = incoming[which, other, :, span] * weight_ref[which, pl.ds(other, 1), span]
                 high, low = split(term)
                 wide_key = jnp.broadcast_to(
@@ -256,9 +268,9 @@
                     total_mid[...] += added
                 else:
                     total_side[which // 2] += added
-                return inner
-
-            lax.fori_loop(0, chunks, land_chunk, 0)
+            return inner
+
+        lax.fori_loop(0, chunks, land_chunk, 0)
         return carry
 
     lax.fori_loop(low_list, high_list, land, 0)
@@ -277,6 +289,9 @@
             )
             partner_ref[field, :half, base : base + edge] += extra[:, :edge]
             partner_ref[field, half:, base : base + edge] += extra[:, edge:]
+        pltpu.make_async_copy(
+            partner_ref.at[field], partner_hbm.at[field], load_sem.at[field]
+        ).start()
 
     def finish(other, carry):
         for which in range(3):
@@ -289,7 +304,10 @@
         copy.wait_send()
     for side in range(2):
         halo_copy(1 - side).wait_recv()
-        halo_ref[side] = halo_in[side]
+    for field in range(fields):
+        pltpu.make_async_copy(
+            partner_ref.at[field], partner_hbm.at[field], load_sem.at[field]
+        ).wait()
 
 
 def advance_kernel(
@@ -382,7 +400,7 @@
     half = rows // 2
     edge = cols // 4
     lists = (3, comp_total, slots)
-    vmem = pl.BlockSpec(memory_space=pltpu.VMEM)
+    hbm = pl.BlockSpec(memory_space=pl.ANY)
     partner, halo = pl.pallas_call(
         functools.partial(
             exchange_kernel, rows, cols, slots, comp_total, tile_total, fields * levels
@@ -394,12 +412,16 @@
         in_specs=[
             pl.BlockSpec(memory_space=pl.ANY),
             pl.BlockSpec(memory_space=pltpu.SMEM),
-            vmem,
-            vmem,
-            vmem,
+            hbm,
+            hbm,
+            hbm,
         ],
-        out_specs=(vmem, vmem),
+        out_specs=(hbm, hbm),
         scratch_shapes=[
+            pltpu.VMEM(lists, jnp.int32),
+            pltpu.VMEM(lists, jnp.int32),
+            pltpu.VMEM(lists, jnp.float32),
+            pltpu.VMEM((fields, rows, cols), jnp.float32),
             pltpu.VMEM((fields, rows, cols), jnp.float32),
             pltpu.VMEM((2, fields, levels, rows, LANES), jnp.float32),
             pltpu.VMEM((2 * fields * rows, cols), jnp.bfloat16),
@@ -407,22 +429,21 @@
             pltpu.VMEM((3, comp_total, fields, slots), jnp.float32),
             pltpu.VMEM((3, comp_total, fields, slots), jnp.float32),
             pltpu.VMEM((2, rows, LANES), jnp.float32),
-            pltpu.VMEM((2, rows, LANES), jnp.float32),
             pltpu.VMEM((2 * fields * rows, cols), jnp.float32),
             pltpu.VMEM((2, 2 * fields * half, 2 * edge), jnp.float32),
             pltpu.VMEM((cols, LANES), jnp.bfloat16),
-            pltpu.SemaphoreType.DMA((3,)),
+            pltpu.SemaphoreType.DMA((6,)),
             pltpu.SemaphoreType.DMA((3, comp_total)),
             pltpu.SemaphoreType.DMA((3, comp_total)),
             pltpu.SemaphoreType.DMA((2,)),
             pltpu.SemaphoreType.DMA((2,)),
         ],
         compiler_params=pltpu.CompilerParams(
-            collective_id=0, has_side_effects=True, vmem_limit_bytes=48 * 1024 * 1024
+            collective_id=0, has_side_effects=True, vmem_limit_bytes=VMEM_BYTES
         ),
     )(
         state,
-        margin_count.reshape(3, comp_total),
+        margin_count.reshape(3, 1, comp_total),
         margin_row.reshape(lists),
         margin_col.reshape(lists),
         margin_weight.reshape(lists),

time: 47.3 us -> 32.8 us (0.69)
  Pallas kernels: 39.9 us -> 31.8 us
  local copies, waits for them, and re-layouts: 6.37 us -> 0 us
    pallas_call x1, Pallas kernels: 31.7 us -> 23.6 us  [shards(): pl.pallas_call(functools.partial(exchange_kernel, rows, cols, slots, comp...]
    unnamed x13 -> x0, local copies, waits for them, and re-layouts: 6.37 us -> none
where the time goes in v2:
time: 32.8 us; the launch traced here: 32.5 us
  Pallas kernels  31.8 us (97%)
  between operations  0.64 us (2%)
    pallas_call x1, Pallas kernels, shards(): pl.pallas_call(functools.partial(exchange_kernel, rows, cols, slots, comp...  23.6 us
    pallas_call x1, Pallas kernels, shards(): pl.pallas_call(advance_kernel, grid=(rows // block,), out_shape=(jax.Shap...  8.25 us

profile of v2, /device:TPU:5, one launch (start us, length us, event | category | flops | bytes accessed | tf_op | source)
XLA Modules:
  0.0 32.5 jit_solution(10760716011618067315)
XLA Ops:
  0.6 23.6 %shard_map.104 = (f32[2,64,512]{2,1,0:T(8,128)}, f32[2,64,128]{2,1,0:T(8,128)}) custom-call(f32[2,8,64,512]{3,2,1,0:T(8,128)} %state_ref.3, s32[3,1,4]{2,1,0:T(1,128)} %bitcast.7, s32[3,4,4096]{2,1,0:T(4,128)} %bitcast.4, s32[3,4,4096]{2,1,0:T(4,128)} %bitcast.5, f32[3,4,4096]{2,1,0:T(4,128)} %bitcast.6), custom_call_target="tpu_custom_call" | custom-call | tf_op jit(solution)/shard_map/pallas_call | solution.py:404
  24.2 8.2 %shard_map.105 = (f32[2,8,64,512]{3,2,1,0:T(8,128)}, f32[2,64,512]{2,1,0:T(8,128)}) custom-call(f32[2,8,64,512]{3,2,1,0:T(8,128)} %state_ref.3, f32[8,64]{1,0:T(8,128)} %courant_ref.1, f32[7,64]{1,0:T(8,128)} %mixing_ref.1, f32[64,512]{1,0:T(8,128)} %exchange_ref.1, s32[64,512]{1,0:T(8,128)} %sea_ref.1, f32[2,64,128]{2,1,0:T(8,128)} %get-tuple-element.4.halo_ref, ...), custom_call_target="tpu_custom_call" | custom-call | tf_op jit(solution)/shard_map/pallas_call | solution.py:453

commit v3 on v2

--- a/solution.py
+++ b/solution.py
@@ -15,7 +15,7 @@
 
 
 def chunk_of(slot_count):
-    for width in (1024, 512, 256):
+    for width in (2048, 1024, 512, 256):
         if slot_count % width == 0:
             return width
     return slot_count
@@ -79,23 +79,38 @@
     total_mid,
     total_side,
     iota_ref,
+    far_surface,
+    far_row,
+    far_col,
+    far_weight,
+    far_mid,
+    far_side,
+    share_out,
+    share_in,
     load_sem,
     send_sem,
     recv_sem,
     halo_send_sem,
     halo_recv_sem,
+    far_send_sem,
+    far_recv_sem,
 ):
     comp = lax.axis_index("comp")
     tile = lax.axis_index("tile")
-    ocean = comp == comp_total - 1
+    sea = comp_total - 1
+    aide = comp_total - 2
+    ocean = comp == sea
+    helper = comp == aide
     tiles = [lax.rem(tile + offset + tile_total, tile_total) for offset in (-1, 0, 1)]
     fields = surface.shape[0]
     half = row_count // 2
     edge = col_count // 4
     width = chunk_of(slot_count)
     chunks = slot_count // width
-    low_list = jnp.where(ocean, 0, comp_total - 1)
-    high_list = jnp.where(ocean, comp_total - 1, comp_total)
+    low_list = jnp.where(ocean, 0, sea)
+    high_list = jnp.where(ocean, aide, comp_total)
+    low_greet = jnp.where(helper, sea, low_list)
+    high_greet = jnp.where(helper, sea, high_list)
 
     load_surface = pltpu.make_async_copy(state_ref.at[:, 0], surface, load_sem.at[0])
     load_surface.start()
@@ -125,27 +140,72 @@
             )
         return carry
 
-    lax.fori_loop(low_list, high_list, greet, 0)
+    lax.fori_loop(low_greet, high_greet, greet, 0)
+
+    @pl.when(ocean)
+    def _():
+        pl.semaphore_signal(barrier, inc=1, device_id=(aide, tile), device_id_type=MESH)
+
+    @pl.when(helper)
+    def _():
+        pl.semaphore_signal(barrier, inc=1, device_id=(sea, tile), device_id_type=MESH)
 
     iota_ref[...] = (lax.broadcasted_iota(jnp.int32, iota_ref.shape, 0) - SHIFT).astype(
         jnp.float32
     ).astype(jnp.bfloat16)
     load_surface.wait()
-    for field in range(fields):
-        value = surface[field]
-        high, low = split(value)
-        for index, piece in ((field, high), (fields + field, low)):
-            table_mid[index * row_count : (index + 1) * row_count, :] = piece
-            for side, base in ((0, 0), (1, col_count - edge)):
-                table_side[side, index * half : (index + 1) * half, :] = jnp.concatenate(
-                    [piece[:half, base : base + edge], piece[half:, base : base + edge]], axis=1
-                )
-    total_mid[...] = jnp.zeros_like(total_mid)
-    total_side[...] = jnp.zeros_like(total_side)
-
+
+    def build_tables(source, mid, side_tables):
+        for field in range(fields):
+            high, low = split(source[field])
+            for index, piece in ((field, high), (fields + field, low)):
+                mid[index * row_count : (index + 1) * row_count, :] = piece
+                for side, base in ((0, 0), (1, col_count - edge)):
+                    side_tables[side, index * half : (index + 1) * half, :] = jnp.concatenate(
+                        [piece[:half, base : base + edge], piece[half:, base : base + edge]],
+                        axis=1,
+                    )
+
+    build_tables(surface, table_mid, table_side)
     for load in list_loads:
         load.wait()
-    pl.semaphore_wait(barrier, 2 + 3 * (high_list - low_list))
+    pl.semaphore_wait(
+        barrier,
+        2 + 3 * (high_greet - low_greet) + jnp.where(ocean | helper, 1, 0),
+    )
+
+    far_copies = []
+    for place, (source, target) in enumerate(
+        (
+            (surface, far_surface),
+            (row_ref, far_row),
+            (col_ref, far_col),
+            (weight_ref, far_weight),
+        )
+    ):
+        far_copies.append(
+            pltpu.make_async_remote_copy(
+                src_ref=source,
+                dst_ref=target,
+                send_sem=far_send_sem.at[place],
+                recv_sem=far_recv_sem.at[place],
+                device_id=(aide, tile),
+                device_id_type=MESH,
+            )
+        )
+    share_copy = pltpu.make_async_remote_copy(
+        src_ref=share_out,
+        dst_ref=share_in,
+        send_sem=far_send_sem.at[4],
+        recv_sem=far_recv_sem.at[4],
+        device_id=(sea, tile),
+        device_id_type=MESH,
+    )
+
+    @pl.when(ocean)
+    def _():
+        for copy in far_copies:
+            copy.start()
 
     def copy_of(which, other):
         return pltpu.make_async_remote_copy(
@@ -153,8 +213,23 @@
             dst_ref=incoming.at[2 - which, comp],
             send_sem=send_sem.at[which, other],
             recv_sem=recv_sem.at[2 - which, comp],
-            device_id=(other, tiles[which]),
+            device_id=(jnp.where(helper, aide, other), tiles[which]),
             device_id_type=MESH,
+        )
+
+    def aide_copy(which):
+        return pltpu.make_async_remote_copy(
+            src_ref=outgoing.at[which, aide],
+            dst_ref=incoming.at[2 - which, sea],
+            send_sem=send_sem.at[which, aide],
+            recv_sem=recv_sem.at[2 - which, sea],
+            device_id=(aide, tiles[which]),
+            device_id_type=MESH,
+        )
+
+    def own_copy(place, source, target):
+        return pltpu.make_async_copy(
+            outgoing.at[1, source], incoming.at[1, target], load_sem.at[3 + place]
         )
 
     def landing_of(which, other):
@@ -167,39 +242,61 @@
             device_id_type=MESH,
         )
 
-    def pick(other, carry):
+    def pick_lists(other, rows_of, cols_of, mid, side_tables, masked):
         def pick_chunk(piece, inner):
             start = pl.multiple_of(piece * width, width)
             span = pl.ds(start, width)
             live_slot = lax.broadcasted_iota(jnp.int32, (1, width), 1) + start
             for which in (1, 0, 2):
-                row = row_ref[which, pl.ds(other, 1), span]
-                col = col_ref[which, pl.ds(other, 1), span]
+                row = rows_of[which, pl.ds(other, 1), span]
+                col = cols_of[which, pl.ds(other, 1), span]
                 key, inside = keys_of(which, row, col, row_count, col_count)
                 if which == 1:
-                    table, depth, rows = table_mid[...], col_count, row_count
+                    table, depth, rows = mid[...], col_count, row_count
                 else:
-                    table, depth, rows = table_side[which // 2], 2 * edge, half
+                    table, depth, rows = side_tables[which // 2], 2 * edge, half
                 picked = jnp.dot(
                     table, one_hot(iota_ref, key, depth), preferred_element_type=jnp.float32
                 )
                 match = lax.broadcasted_iota(jnp.int32, (rows, width), 0) == inside
-                live = live_slot < count_ref[which, 0, other]
+                if masked:
+                    live = live_slot < count_ref[which, 0, other]
                 for field in range(fields):
                     both = (
                         picked[field * rows : (field + 1) * rows]
                         + picked[(fields + field) * rows : (fields + field + 1) * rows]
                     )
                     value = jnp.sum(jnp.where(match, both, 0.0), axis=0, keepdims=True)
-                    outgoing[which, other, field : field + 1, span] = jnp.where(live, value, 0.0)
+                    if masked:
+                        value = jnp.where(live, value, 0.0)
+                    outgoing[which, other, field : field + 1, span] = value
             return inner
 
         lax.fori_loop(0, chunks, pick_chunk, 0)
-        for which in range(3):
+
+    def pick(other, carry):
+        pick_lists(other, row_ref, col_ref, table_mid, table_side, True)
+        for which in (0, 2):
             copy_of(which, other).start()
+
+        @pl.when(jnp.logical_not(helper))
+        def _():
+            copy_of(1, other).start()
+
         return carry
 
     lax.fori_loop(low_list, high_list, pick, 0)
+
+    @pl.when(helper)
+    def _():
+        own_copy(0, sea, aide).start()
+        for copy in far_copies:
+            copy.wait_recv()
+        build_tables(far_surface, far_mid, far_side)
+        pick_lists(aide, far_row, far_col, far_mid, far_side, False)
+        for which in (0, 2):
+            aide_copy(which).start()
+        own_copy(1, aide, sea).start()
 
     for load in loads:
         load.wait()
@@ -226,19 +323,19 @@
     for side in range(2):
         halo_copy(side).start()
 
-    def land(other, carry):
-        for which in range(3):
-            landing_of(which, other).wait_recv()
-
+    def land_lists(other, rows_of, cols_of, weights_of, masked):
         def land_chunk(piece, inner):
             start = pl.multiple_of(piece * width, width)
             span = pl.ds(start, width)
+            live_slot = lax.broadcasted_iota(jnp.int32, (1, width), 1) + start
             for which in (1, 0, 2):
-                row = row_ref[which, pl.ds(other, 1), span]
-                col = col_ref[which, pl.ds(other, 1), span]
+                row = rows_of[which, pl.ds(other, 1), span]
+                col = cols_of[which, pl.ds(other, 1), span]
                 key, inside = keys_of(which, row, col, row_count, col_count)
                 depth, rows = (col_count, row_count) if which == 1 else (2 * edge, half)
-                term = incoming[which, other, :, span] * weight_ref[which, pl.ds(other, 1), span]
+                term = incoming[which, other, :, span] * weights_of[which, pl.ds(other, 1), span]
+                if masked:
+                    term = jnp.where(live_slot < count_ref[which, 0, other], term, 0.0)
                 high, low = split(term)
                 wide_key = jnp.broadcast_to(
                     inside.astype(jnp.float32) - SHIFT, (16, width)
@@ -271,34 +368,88 @@
             return inner
 
         lax.fori_loop(0, chunks, land_chunk, 0)
+
+    def land(other, carry):
+        for which in (0, 2):
+            landing_of(which, other).wait_recv()
+
+        @pl.when(jnp.logical_not(helper))
+        def _():
+            landing_of(1, other).wait_recv()
+
+        land_lists(other, row_ref, col_ref, weight_ref, True)
         return carry
 
-    lax.fori_loop(low_list, high_list, land, 0)
-
-    for field in range(fields):
+    def clear_totals():
+        total_mid[...] = jnp.zeros_like(total_mid)
+        total_side[...] = jnp.zeros_like(total_side)
+
+    def gather_totals(field, target):
         first, second = field, fields + field
-        whole = (
+        target[field] = (
             total_mid[first * row_count : (first + 1) * row_count, :]
             + total_mid[second * row_count : (second + 1) * row_count, :]
         )
-        partner_ref[field] = whole
         for side, base in ((0, 0), (1, col_count - edge)):
             extra = (
                 total_side[side, first * half : (first + 1) * half, :]
                 + total_side[side, second * half : (second + 1) * half, :]
             )
-            partner_ref[field, :half, base : base + edge] += extra[:, :edge]
-            partner_ref[field, half:, base : base + edge] += extra[:, edge:]
+            target[field, :half, base : base + edge] += extra[:, :edge]
+            target[field, half:, base : base + edge] += extra[:, edge:]
+
+    clear_totals()
+
+    @pl.when(helper)
+    def _():
+        own_copy(0, sea, aide).wait()
+        for which in (0, 2):
+            landing_of(which, aide).wait_recv()
+        land_lists(aide, far_row, far_col, far_weight, False)
+        for field in range(fields):
+            gather_totals(field, share_out)
+        share_copy.start()
+        clear_totals()
+        own_copy(1, aide, sea).wait()
+
+    lax.fori_loop(low_list, high_list, land, 0)
+
+    for field in range(fields):
+        gather_totals(field, partner_ref)
+
+    @pl.when(ocean)
+    def _():
+        share_copy.wait_recv()
+        partner_ref[...] += share_in[...]
+
+    for field in range(fields):
         pltpu.make_async_copy(
             partner_ref.at[field], partner_hbm.at[field], load_sem.at[field]
         ).start()
 
     def finish(other, carry):
-        for which in range(3):
+        for which in (0, 2):
             copy_of(which, other).wait_send()
+
+        @pl.when(jnp.logical_not(helper))
+        def _():
+            copy_of(1, other).wait_send()
+
         return carry
 
     lax.fori_loop(low_list, high_list, finish, 0)
+
+    @pl.when(helper)
+    def _():
+        for which in (0, 2):
+            aide_copy(which).wait_send()
+        share_copy.wait_send()
+
+    @pl.when(ocean)
+    def _():
+        for copy in far_copies:
+            copy.wait_send()
+
     for side in range(2):
         copy = halo_copy(side)
         copy.wait_send()
@@ -348,19 +499,25 @@
             ends = jnp.where(lane < LANES // 2, east, west)
             columns.append(jnp.concatenate([state_ref[field, level], ends], axis=1))
         for substep in range(SUBSTEPS):
+            span_out = total if substep < SUBSTEPS - 1 else cols
             moved = []
             for level in range(levels):
-                c = jnp.broadcast_to(speeds[:, level : level + 1], (rows, total))
                 q = columns[level]
-                left = pltpu.roll(q, 1, 1)
-                right = pltpu.roll(q, total - 1, 1)
-                moved.append(q - 0.5 * c * (right - left) + 0.5 * c * c * (right - 2.0 * q + left))
+                left = pltpu.roll(q, 1, 1)[:, :span_out]
+                right = pltpu.roll(q, total - 1, 1)[:, :span_out]
+                c = speeds[:, level : level + 1]
+                half_c = 0.5 * c
+                half_square = half_c * c
+                from_left = jnp.broadcast_to(half_c + half_square, (rows, span_out))
+                from_right = jnp.broadcast_to(half_square - half_c, (rows, span_out))
+                own = jnp.broadcast_to(1.0 - 2.0 * half_square, (rows, span_out))
+                moved.append(own * q[:, :span_out] + from_left * left + from_right * right)
             columns = []
             flux = None
             for level in range(levels):
                 value = moved[level]
                 if level < levels - 1:
-                    m = jnp.broadcast_to(mixes[:, level : level + 1], (rows, total))
+                    m = jnp.broadcast_to(mixes[:, level : level + 1], (rows, span_out))
                     above = m * (moved[level + 1] - moved[level])
                     value = value + above
                 if level > 0:
@@ -369,8 +526,8 @@
                     flux = above
                 columns.append(value)
         for level in range(1, levels):
-            new_ref[field, level] = columns[level][:, :cols]
-        surface.append(columns[0][:, :cols])
+            new_ref[field, level] = columns[level]
+        surface.append(columns[0])
     rate = exchange_ref[...] * sea_ref[...].astype(jnp.float32)
     first, second = surface
     far = partner_in_ref[0]
@@ -432,11 +589,21 @@
             pltpu.VMEM((2 * fields * rows, cols), jnp.float32),
             pltpu.VMEM((2, 2 * fields * half, 2 * edge), jnp.float32),
             pltpu.VMEM((cols, LANES), jnp.bfloat16),
+            pltpu.VMEM((fields, rows, cols), jnp.float32),
+            pltpu.VMEM(lists, jnp.int32),
+            pltpu.VMEM(lists, jnp.int32),
+            pltpu.VMEM(lists, jnp.float32),
+            pltpu.VMEM((2 * fields * rows, cols), jnp.bfloat16),
+            pltpu.VMEM((2, 2 * fields * half, 2 * edge), jnp.bfloat16),
+            pltpu.VMEM((fields, rows, cols), jnp.float32),
+            pltpu.VMEM((fields, rows, cols), jnp.float32),
             pltpu.SemaphoreType.DMA((6,)),
             pltpu.SemaphoreType.DMA((3, comp_total)),
             pltpu.SemaphoreType.DMA((3, comp_total)),
             pltpu.SemaphoreType.DMA((2,)),
             pltpu.SemaphoreType.DMA((2,)),
+            pltpu.SemaphoreType.DMA((5,)),
+            pltpu.SemaphoreType.DMA((5,)),
         ],
         compiler_params=pltpu.CompilerParams(
             collective_id=0, has_side_effects=True, vmem_limit_bytes=VMEM_BYTES
@@ -448,7 +615,7 @@
         margin_col.reshape(lists),
         margin_weight.reshape(lists),
     )
-    block = 8
+    block = 16
     plane = pl.BlockSpec((block, cols), lambda i: (i, 0))
     return pl.pallas_call(
         advance_kernel,

time: 32.8 us -> 25.1 us (0.77)
  Pallas kernels: 31.8 us -> 24.2 us
    pallas_call x1, Pallas kernels: 23.6 us -> 17.8 us  [shards(): pl.pallas_call(functools.partial(exchange_kernel, rows, cols, slots, comp...]
    pallas_call x1, Pallas kernels: 8.25 us -> 6.42 us  [shards(): pl.pallas_call(advance_kernel, grid=(rows // block,), out_shape=(jax.Shap...]
where the time goes in v3:
time: 25.1 us; the launch traced here: 24.8 us
  Pallas kernels  24.2 us (96%)
  between operations  0.64 us (3%)
    pallas_call x1, Pallas kernels, shards(): pl.pallas_call(functools.partial(exchange_kernel, rows, cols, slots, comp...  17.8 us
    pallas_call x1, Pallas kernels, shards(): pl.pallas_call(advance_kernel, grid=(rows // block,), out_shape=(jax.Shap...  6.42 us

profile of v3, /device:TPU:5, one launch (start us, length us, event | category | flops | bytes accessed | tf_op | source)
XLA Modules:
  0.0 24.8 jit_solution(8411641485047588311)
XLA Ops:
  0.6 17.8 %shard_map.104 = (f32[2,64,512]{2,1,0:T(8,128)}, f32[2,64,128]{2,1,0:T(8,128)}) custom-call(f32[2,8,64,512]{3,2,1,0:T(8,128)} %state_ref.3, s32[3,1,4]{2,1,0:T(1,128)} %bitcast.7, s32[3,4,4096]{2,1,0:T(4,128)} %bitcast.4, s32[3,4,4096]{2,1,0:T(4,128)} %bitcast.5, f32[3,4,4096]{2,1,0:T(4,128)} %bitcast.6), custom_call_target="tpu_custom_call" | custom-call | tf_op jit(solution)/shard_map/pallas_call | solution.py:561
  18.4 6.4 %shard_map.105 = (f32[2,8,64,512]{3,2,1,0:T(8,128)}, f32[2,64,512]{2,1,0:T(8,128)}) custom-call(f32[2,8,64,512]{3,2,1,0:T(8,128)} %state_ref.3, f32[8,64]{1,0:T(8,128)} %courant_ref.1, f32[7,64]{1,0:T(8,128)} %mixing_ref.1, f32[64,512]{1,0:T(8,128)} %exchange_ref.1, s32[64,512]{1,0:T(8,128)} %sea_ref.1, f32[2,64,128]{2,1,0:T(8,128)} %get-tuple-element.4.halo_ref, ...), custom_call_target="tpu_custom_call" | custom-call | tf_op jit(solution)/shard_map/pallas_call | solution.py:620

commit v4 on v3

--- a/solution.py
+++ b/solution.py
@@ -167,6 +167,22 @@
                     )
 
     build_tables(surface, table_mid, table_side)
+    def clear_totals():
+        total_mid[...] = jnp.zeros_like(total_mid)
+        total_side[...] = jnp.zeros_like(total_side)
+
+    clear_totals()
+    for load in loads:
+        load.wait()
+    lane = lax.broadcasted_iota(jnp.int32, (row_count, LANES), 1)
+    for side in range(2):
+        packed = jnp.zeros((row_count, LANES), jnp.float32)
+        for place in range(fl_count):
+            level = edges[side, place // (fl_count // fields), place % (fl_count // fields)]
+            shift = SUBSTEPS * place + (0 if side == 0 else SUBSTEPS)
+            moved = level if shift == 0 else pltpu.roll(level, shift, 1)
+            packed = jnp.where(lane // SUBSTEPS == place, moved, packed)
+        halo_out[side] = packed
     for load in list_loads:
         load.wait()
     pl.semaphore_wait(
@@ -297,18 +313,6 @@
         for which in (0, 2):
             aide_copy(which).start()
         own_copy(1, aide, sea).start()
-
-    for load in loads:
-        load.wait()
-    lane = lax.broadcasted_iota(jnp.int32, (row_count, LANES), 1)
-    for side in range(2):
-        packed = jnp.zeros((row_count, LANES), jnp.float32)
-        for place in range(fl_count):
-            level = edges[side, place // (fl_count // fields), place % (fl_count // fields)]
-            shift = SUBSTEPS * place + (0 if side == 0 else SUBSTEPS)
-            moved = level if shift == 0 else pltpu.roll(level, shift, 1)
-            packed = jnp.where(lane // SUBSTEPS == place, moved, packed)
-        halo_out[side] = packed
 
     def halo_copy(side):
         return pltpu.make_async_remote_copy(
@@ -380,10 +384,6 @@
         land_lists(other, row_ref, col_ref, weight_ref, True)
         return carry
 
-    def clear_totals():
-        total_mid[...] = jnp.zeros_like(total_mid)
-        total_side[...] = jnp.zeros_like(total_side)
-
     def gather_totals(field, target):
         first, second = field, fields + field
         target[field] = (
@@ -397,8 +397,6 @@
             )
             target[field, :half, base : base + edge] += extra[:, :edge]
             target[field, half:, base : base + edge] += extra[:, edge:]
-
-    clear_totals()
 
     @pl.when(helper)
     def _():

time: 25.1 us -> 25.6 us (1.020)
  the two profiles are of different devices: /device:TPU:5 before, /device:TPU:1 now
where the time goes in v4:
time: 25.6 us; the launch traced here: 25.3 us
  Pallas kernels  24.7 us (96%)
  between operations  0.64 us (2%)
    pallas_call x1, Pallas kernels, shards(): pl.pallas_call(functools.partial(exchange_kernel, rows, cols, slots, comp...  18.3 us
    pallas_call x1, Pallas kernels, shards(): pl.pallas_call(advance_kernel, grid=(rows // block,), out_shape=(jax.Shap...  6.42 us

profile of v4, /device:TPU:1, one launch (start us, length us, event | category | flops | bytes accessed | tf_op | source)
XLA Modules:
  0.0 25.3 jit_solution(9207266893271639650)
XLA Ops:
  0.6 18.3 %shard_map.104 = (f32[2,64,512]{2,1,0:T(8,128)}, f32[2,64,128]{2,1,0:T(8,128)}) custom-call(f32[2,8,64,512]{3,2,1,0:T(8,128)} %state_ref.3, s32[3,1,4]{2,1,0:T(1,128)} %bitcast.7, s32[3,4,4096]{2,1,0:T(4,128)} %bitcast.4, s32[3,4,4096]{2,1,0:T(4,128)} %bitcast.5, f32[3,4,4096]{2,1,0:T(4,128)} %bitcast.6), custom_call_target="tpu_custom_call" | custom-call | tf_op jit(solution)/shard_map/pallas_call | solution.py:559
  18.9 6.4 %shard_map.105 = (f32[2,8,64,512]{3,2,1,0:T(8,128)}, f32[2,64,512]{2,1,0:T(8,128)}) custom-call(f32[2,8,64,512]{3,2,1,0:T(8,128)} %state_ref.3, f32[8,64]{1,0:T(8,128)} %courant_ref.1, f32[7,64]{1,0:T(8,128)} %mixing_ref.1, f32[64,512]{1,0:T(8,128)} %exchange_ref.1, s32[64,512]{1,0:T(8,128)} %sea_ref.1, f32[2,64,128]{2,1,0:T(8,128)} %get-tuple-element.4.halo_ref, ...), custom_call_target="tpu_custom_call" | custom-call | tf_op jit(solution)/shard_map/pallas_call | solution.py:618
